TPU v7x, 256 devices: a whole 4x4x8 slice. The times are simulated.
256 devices in a mesh: expert: 64 (over z, y, core), tensor: 4 (over x).
Axes of the slice: x: 4, y: 4, z: 8, core: 2. Of those that a mesh axis runs over, the one named last changes fastest.
Arguments:
- context: bfloat16 [8192, 4096], P('expert', 'tensor'), may hold values from -6 to 6
- residual_in: bfloat16 [8192, 4096], P('expert')
- out_weight: bfloat16 [4096, 4096], P('tensor', 'expert'), may hold values from -0.09375 to 0.09375
- norm_gain: bfloat16 [4096], replicated, may hold values from 0.099609375 to 1.8984375
- expert_ids: int32 [8192, 8], P('expert'), may hold values from 0 to 63, all different within a row; in each aligned block of 128 rows (0 to 127, 128 to 255, ...) at most 18 rows name the same one
- gate_weights: float32 [8192, 8], P('expert'), may hold values from 0.1 to 1
- gate_matrix: bfloat16 [64, 4096, 1536], P('expert', None, 'tensor'), may hold values from -0.09375 to 0.09375
- lift_matrix: bfloat16 [64, 4096, 1536], P('expert', None, 'tensor'), may hold values from -0.09375 to 0.09375
- down_matrix: bfloat16 [64, 1536, 4096], P('expert', 'tensor'), may hold values from -0.15625 to 0.15625
Outputs:
- layer_out: bfloat16 [8192, 4096], P('expert', 'tensor')
Inputs may be any that keep to these rules, and one draw needn't show every extreme that they name: `expert_ids`: each row names 8 different experts. Within each aligned block of 128 rows (the rows of one index of the expert axis) no expert is named more than 18 times, a bound that some block reaches.
All inputs are finite; a program needn't handle non-finite values.
Results may differ from a plain program's by a relative error of at most 0.009.
Values may be sent and summed in bfloat16 or wider, within the bound.
No kernel may reach another device: no remote copies, remote signals or barrier semaphores. Data moves between devices by JAX's collectives and lax.ppermute only.
A program may use at most 128 MiB of HBM per device.

v0:
```python
import jax
import jax.numpy as jnp
from jax import lax
from jax.sharding import PartitionSpec as P

epsilon = 1e-06


def body(
    context,
    residual_in,
    out_weight,
    norm_gain,
    expert_ids,
    gate_weights,
    gate_matrix,
    lift_matrix,
    down_matrix,
):
    tokens_here, model_width = residual_in.shape
    top_count = expert_ids.shape[1]
    share_width = model_width // lax.axis_size("tensor")
    column_start = lax.axis_index("tensor") * share_width
    experts_all = lax.axis_size("expert") * gate_matrix.shape[0]
    capacity = min(tokens_here, max(2, tokens_here * top_count * 9 // (8 * experts_all)))
    attention_part = jnp.dot(
        context,
        lax.all_gather(out_weight, "expert", axis=1, tiled=True),
        preferred_element_type=jnp.float32,
    )
    attention_out = lax.psum(attention_part, "tensor")
    hidden_state = (residual_in.astype(jnp.float32) + attention_out).astype(jnp.bfloat16)
    widened = hidden_state.astype(jnp.float32)
    squares_mean = jnp.mean(widened * widened, axis=1, keepdims=True)
    normed_full = (
        widened * lax.rsqrt(squares_mean + epsilon) * norm_gain.astype(jnp.float32)
    ).astype(jnp.bfloat16)
    hidden_share = lax.dynamic_slice_in_dim(hidden_state, column_start, share_width, 1)
    flat_ids = expert_ids.reshape(-1)
    onehot_table = (flat_ids[:, None] == jnp.arange(experts_all, dtype=jnp.int32)[None, :]).astype(
        jnp.int32
    )
    earlier = jnp.cumsum(onehot_table, axis=0) - onehot_table
    slot_index = jnp.sum(earlier * onehot_table, axis=1)
    destination = flat_ids * capacity + slot_index
    token_index = jnp.arange(tokens_here * top_count, dtype=jnp.int32) // top_count
    source_width = normed_full.shape[1]
    buffer_rows = jnp.zeros((experts_all * capacity, source_width), jnp.bfloat16)
    buffer_rows = buffer_rows.at[destination].set(normed_full[token_index])
    buffer_rows = buffer_rows.reshape(experts_all, capacity, source_width)
    received = lax.all_to_all(buffer_rows, "expert", split_axis=0, concat_axis=0, tiled=True)
    senders = received.shape[0]
    slots_here = received.shape[1]
    flat_rows = received.reshape(senders * slots_here, model_width)
    gate_values = jnp.dot(flat_rows, gate_matrix[0], preferred_element_type=jnp.float32)
    lift_values = jnp.dot(flat_rows, lift_matrix[0], preferred_element_type=jnp.float32)
    activation = (jax.nn.silu(gate_values) * lift_values).astype(jnp.bfloat16)
    partial_out = jnp.dot(activation, down_matrix[0], preferred_element_type=jnp.float32)
    expert_partial = partial_out.reshape(senders, slots_here, model_width)
    expert_share = lax.psum_scatter(
        expert_partial.astype(jnp.bfloat16), "tensor", scatter_dimension=2, tiled=True
    )
    returned = lax.all_to_all(expert_share, "expert", split_axis=0, concat_axis=0, tiled=True)
    picked = returned.reshape(experts_all * capacity, share_width)[destination]
    picked = picked.reshape(tokens_here, top_count, share_width)
    moe_share = jnp.sum(gate_weights[:, :, None] * picked.astype(jnp.float32), axis=1)
    return (hidden_share.astype(jnp.float32) + moe_share).astype(jnp.bfloat16)


def solution(mesh):
    placed = (
        P("expert", "tensor"),
        P("expert", None),
        P("tensor", "expert"),
        P(),
        P("expert", None),
        P("expert", None),
        P("expert", None, "tensor"),
        P("expert", None, "tensor"),
        P("expert", "tensor", None),
    )
    return jax.shard_map(
        body, mesh=mesh, in_specs=placed, out_specs=P("expert", "tensor"), check_vma=False
    )
```

profile of v0, /device:TPU:8, one launch (start us, length us, event | category | flops | bytes accessed | tf_op | source)
XLA Modules:
  0.0 744.2 jit_solution(13246930377981361659)
XLA Ops:
  6.5 0.7 all-gather.2.cloned.1.call-update
  7.3 87.5 %all-gather.2.cloned.1.call-done = bf16[1024,4096]{0,1:T(8,128)(2,1)} async-done(((bf16[1024,64]{0,1:T(8,128)(2,1)}), bf16[1024,4096]{0,1:T(8,128)(2,1)}) %all-gather.2.cloned.1.call-update) | async-done | bytes 8388624 | tf_op jit(solution)/shard_map/all_gather | solution.py:28
  94.8 7.7 %fusion.18 = f32[128,4096]{1,0:T(8,128)} fusion(bf16[128,1024]{1,0:T(8,128)(2,1)} %param.9, bf16[1024,4096]{0,1:T(8,128)(2,1)} %all-gather.2.cloned.1.call-done), kind=kOutput, calls=%fused_computation.40 | convolution fusion | flops 1073741824 | bytes 10747904 | tf_op jit(solution)/shard_map/dot_general | solution.py:26
  102.6 0.1 copy.22
  102.9 0.7 fusion.17
  103.6 31.1 %reduce-window.6 = s32[64,8,128]{2,1,0:T(8,128)S(1)} reduce-window(s32[64,8,128]{2,1,0:T(8,128)} %fusion.17, s32[]{:T(128)} %constant.17.clone.1), window={size=1x1x128 pad=0_0x0_0x127_0}, to_apply=%region_1.0 | reduce-window | flops 8323072 | bytes 524292 | tf_op jit(solution)/shard_map/reduce-window
  134.7 0.8 slice.12
  135.6 1.1 copy.24
  136.8 0.1 copy.21
  136.9 0.1 mul.60
  137.0 0.1 broadcast_add_fusion
  137.3 27.9 %all-reduce.2.cloned.1.call-done = f32[128,4096]{1,0:T(8,128)} async-done(((f32[128,4096]{1,0:T(8,128)}), f32[128,4096]{1,0:T(8,128)}) %all-reduce.2.cloned.1.call-update) | async-done | bytes 2097168 | tf_op jit(solution)/shard_map/psum | solution.py:31
  165.1 2.3 fusion.10
  167.4 1.1 copy-done.2
  168.5 1.4 fusion.12
  169.9 16.4 %gather_fusion = bf16[1024,4096]{1,0:T(8,128)(2,1)} fusion(bf16[128,4096]{1,0:T(8,128)(2,1)} %fusion.12, s32[1024]{0:T(1024)S(1)} %broadcast_clamp_fusion.1), kind=kCustom, calls=%fused_computation | custom fusion | bytes 16781312 | tf_op jit(solution)/shard_map/gather | solution.py:49
  186.3 18.2 %scatter_custom_fusion = bf16[1152,4096]{1,0:T(8,128)(2,1)} fusion(s32[1024]{0:T(1024)S(1)} %bitcast.43, bf16[1024,4096]{1,0:T(8,128)(2,1)} %gather_fusion, bf16[]{:T(256)} %constant.38.clone.1), kind=kCustom, calls=%fused_computation.4 | custom fusion | bytes 9437696 | tf_op jit(solution)/shard_map/scatter | solution.py:49
  204.5 13.9 %reshape.114 = bf16[64,18,4096]{2,1,0:T(8,128)(2,1)} reshape(bf16[1152,4096]{1,0:T(8,128)(2,1)} %scatter_custom_fusion) | data formatting | bytes 18874368 | tf_op jit(solution)/shard_map/reshape | solution.py:50
  218.4 286.6 %all_to_all.10 = bf16[64,18,4096]{2,1,0:T(8,128)(2,1)} all-to-all(bf16[64,18,4096]{2,1,0:T(8,128)(2,1)} %reshape.114), channel_id=1, replica_groups=mesh['expert'=64,'tensor'=4] {'expert'}, dimensions={0} | all-to-all | bytes 18874368 | tf_op jit(solution)/shard_map/all_to_all | solution.py:51
  505.0 14.2 %reshape.115 = bf16[1152,4096]{1,0:T(8,128)(2,1)} reshape(bf16[64,18,4096]{2,1,0:T(8,128)(2,1)} %all_to_all.10) | data formatting | bytes 18874368 | tf_op jit(solution)/shard_map/reshape | solution.py:54
  519.2 8.7 %fusion.5 = f32[1152,384]{1,0:T(8,128)S(1)} fusion(bf16[1152,4096]{1,0:T(8,128)(2,1)} %reshape.115, bf16[1,4096,384]{2,1,0:T(8,128)(2,1)} %param.15), kind=kOutput, calls=%fused_computation.11 | convolution fusion | flops 3623878656 | bytes 14352384 | tf_op jit(solution)/shard_map/dot_general | solution.py:55
  527.9 6.2 fusion.7
  534.1 2.2 dot_general.17
  536.3 8.7 %convolution_convert_fusion = bf16[64,18,4096]{2,0,1:T(8,128)(2,1)} fusion(bf16[1,384,4096]{2,1,0:T(8,128)(2,1)S(1)} %copy-done, bf16[64,18,384]{2,1,0:T(8,128)(2,1)} %dot_general.17), kind=kOutput, calls=%fused_computation.3 | convolution fusion | flops 3628597248 | bytes 13467648 | tf_op jit(solution)/shard_map/dot_general | solution.py:58
  545.0 86.4 %reduce-scatter.2.cloned.1.call-done = bf16[64,18,1024]{2,0,1:T(8,128)(2,1)} async-done(((bf16[64,18,4096]{2,0,1:T(8,128)(2,1)}), bf16[64,18,1024]{2,0,1:T(8,128)(2,1)}) %reduce-scatter.2.cloned.1.call-update) | async-done | bytes 2359312 | tf_op jit(solution)/shard_map/reduce_scatter | solution.py:60
  631.4 4.7 copy.27
  636.2 10.9 %all-to-all-start.1 = ((bf16[64,18,1024]{2,1,0:T(8,128)(2,1)}), bf16[64,18,1024]{2,1,0:T(8,128)(2,1)}, u32[]{:S(2)}, u32[]{:S(2)}) async-start(bf16[64,18,1024]{2,1,0:T(8,128)(2,1)} %copy.27), calls=%async_computation.2 | async-start | bytes 6291456 | tf_op jit(solution)/shard_map/all_to_all | solution.py:63
  647.2 73.5 %all-to-all-done.1 = bf16[64,18,1024]{2,1,0:T(8,128)(2,1)} async-done(((bf16[64,18,1024]{2,1,0:T(8,128)(2,1)}), bf16[64,18,1024]{2,1,0:T(8,128)(2,1)}, u32[]{:S(2)}, u32[]{:S(2)}) %all-to-all-start.1) | async-done | bytes 2359328 | tf_op jit(solution)/shard_map/all_to_all | solution.py:63
  720.7 4.3 reshape.116
  725.0 8.0 %gather_fusion.1 = bf16[1024,1024]{1,0:T(8,128)(2,1)} fusion(bf16[1152,1024]{1,0:T(8,128)(2,1)} %reshape.116, s32[1024]{0:T(1024)S(1)} %broadcast_clamp_fusion), kind=kCustom, calls=%fused_computation.1 | custom fusion | bytes 4198400 | tf_op jit(solution)/shard_map/gather | solution.py:64
  733.0 2.9 fusion.2
  735.9 1.7 add_convert_fusion.1
  (32 shorter events, 0.6 us)
Async XLA Ops:
  6.5 529.8 %copy-start = (bf16[1,384,4096]{2,1,0:T(8,128)(2,1)S(1)}, bf16[1,384,4096]{2,1,0:T(8,128)(2,1)}, u32[]{:S(2)}) copy-start(bf16[1,384,4096]{2,1,0:T(8,128)(2,1)} %param.17) | copy-start | bytes 9437188
  6.5 88.3 %all-gather.2.cloned.1.call-start = ((), (), s32[]{:S(2)}) async-start(), calls=%async_computation.3 | async-start | bytes 8519680 | tf_op jit(solution)/shard_map/all_gather | solution.py:28
  7.3 95.3 %copy-start.3 = (s32[128,8]{0,1:T(8,128)S(1)}, s32[128,8]{0,1:T(8,128)}, u32[]{:S(2)}) copy-start(s32[128,8]{0,1:T(8,128)} %param.13) | copy-start | bytes 12292
  7.3 157.9 %all-reduce.2.cloned.1.call-start = ((), (), s32[]{:S(2)}) async-start(), calls=%async_computation.4 | async-start | bytes 4194304 | tf_op jit(solution)/shard_map/psum | solution.py:31
  102.5 34.5 %copy-start.4 = (bf16[4096]{0:T(1024)(128)(2,1)S(1)}, bf16[4096]{0:T(1024)(128)(2,1)}, u32[]{:S(2)}) copy-start(bf16[4096]{0:T(1024)(128)(2,1)} %param.12) | copy-start | bytes 24580
  102.6 528.9 %reduce-scatter.2.cloned.1.call-start = ((), (), s32[]{:S(2)}) async-start(), calls=%async_computation.5 | async-start | bytes 11796480 | tf_op jit(solution)/shard_map/reduce_scatter | solution.py:60
  167.4 1.1 copy-start.2
  519.2 8.7 %copy-start.1 = (bf16[1152,4096]{1,0:T(8,128)(2,1)S(1)}, bf16[1152,4096]{1,0:T(8,128)(2,1)}, u32[]{:S(2)}) copy-start(bf16[1152,4096]{1,0:T(8,128)(2,1)} %reshape.115) | copy-start | bytes 28311556
  519.2 8.7 %copy-start.6 = (bf16[1,4096,384]{2,1,0:T(8,128)(2,1)S(1)}, bf16[1,4096,384]{2,1,0:T(8,128)(2,1)}, u32[]{:S(2)}) copy-start(bf16[1,4096,384]{2,1,0:T(8,128)(2,1)} %param.16) | copy-start | bytes 9437188
  636.2 10.9 %copy-start.5 = (f32[128,8]{0,1:T(8,128)S(1)}, f32[128,8]{0,1:T(8,128)}, u32[]{:S(2)}) copy-start(f32[128,8]{0,1:T(8,128)} %param.14) | copy-start | bytes 12292
  636.2 84.5 %all-to-all-start.1 = ((bf16[64,18,1024]{2,1,0:T(8,128)(2,1)}), bf16[64,18,1024]{2,1,0:T(8,128)(2,1)}, u32[]{:S(2)}, u32[]{:S(2)}) async-start(bf16[64,18,1024]{2,1,0:T(8,128)(2,1)} %copy.27), calls=%async_computation.2 | async-start | bytes 6291456 | tf_op jit(solution)/shard_map/all_to_all | solution.py:63
Sparse Core Ops, SparseCore 0:
  10.1 84.6 all-gather.1
  102.7 62.4 all-reduce.1
  545.1 86.2 reduce-scatter.1
where the time goes:
time: 747 us; the launch traced here: 744 us
  blocking collectives  287 us (38%)
  waiting for transfers between devices  276 us (37%)
  local copies, waits for them, and re-layouts  85.7 us (11%)
  other arithmetic  40.4 us (5%)
  matrix products  31.3 us (4%)
  between operations  13.3 us (2%)
  starting transfers between devices  11 us (1%)
    all_to_all x1, blocking collectives, body(): lax.all_to_all(buffer_rows, 'expert', split_axis=0, concat_axis=0, tiled=...  287 us
    all_gather x1, waiting for transfers between devices, body(): lax.all_gather(out_weight, 'expert', axis=1, tiled=True)  87.5 us
    reduce_scatter x1, waiting for transfers between devices, body(): lax.psum_scatter(expert_partial.astype(jnp.bfloat16), 'tensor', scatter_d...  86.4 us
    all_to_all x1, waiting for transfers between devices, body(): lax.all_to_all(expert_share, 'expert', split_axis=0, concat_axis=0, tiled...  73.5 us
    another operation x3, other arithmetic  31.3 us
    psum x1, waiting for transfers between devices, body(): attention_out = lax.psum(attention_part, 'tensor')  27.9 us
    scatter x1, local copies, waits for them, and re-layouts, body(): buffer_rows = buffer_rows.at[destination].set(normed_full[token_index])  18.2 us
    gather x1, local copies, waits for them, and re-layouts, body(): buffer_rows = buffer_rows.at[destination].set(normed_full[token_index])  16.4 us
  transfers between devices with their start and end apart: 4, of which 4 were waited for; matrix products, arithmetic and copies ran while one was open for 5% of the time, Pallas kernels for 0%

commit v1 on v0

--- a/solution.py
+++ b/solution.py
@@ -4,6 +4,12 @@
 from jax.sharding import PartitionSpec as P
 
 epsilon = 1e-06
+
+
+def add_all(x, name):
+    pieces = lax.all_gather(x, name, axis=0, tiled=False)
+    result = pieces.sum(axis=0)
+    return result
 
 
 def body(
@@ -28,7 +34,7 @@
         lax.all_gather(out_weight, "expert", axis=1, tiled=True),
         preferred_element_type=jnp.float32,
     )
-    attention_out = lax.psum(attention_part, "tensor")
+    attention_out = add_all(attention_part, "tensor")
     hidden_state = (residual_in.astype(jnp.float32) + attention_out).astype(jnp.bfloat16)
     widened = hidden_state.astype(jnp.float32)
     squares_mean = jnp.mean(widened * widened, axis=1, keepdims=True)

time: 747 us -> 775 us (1.037)
  waiting for transfers between devices: 276 us -> 299 us
    all_gather x0 -> x1, waiting for transfers between devices: none -> 49.6 us  [add_all(): pieces = lax.all_gather(x, name, axis=0, tiled=False)]
    psum x1 -> x0, waiting for transfers between devices: 27.9 us -> none  [body(): attention_out = lax.psum(attention_part, 'tensor')]
  transfers between devices with their start and end apart: 4 -> 4, of which waited for: 4 -> 4; matrix products, arithmetic and copies ran while one was open for 5% -> 4% of each run, Pallas kernels for 0% -> 0%
where the time goes in v1:
time: 775 us; the launch traced here: 773 us
  waiting for transfers between devices  299 us (39%)
  blocking collectives  287 us (37%)
  local copies, waits for them, and re-layouts  85.7 us (11%)
  other arithmetic  46 us (6%)
  matrix products  31.3 us (4%)
  between operations  13.3 us (2%)
  starting transfers between devices  11 us (1%)
    all_to_all x1, blocking collectives, body(): lax.all_to_all(buffer_rows, 'expert', split_axis=0, concat_axis=0, tiled=...  287 us
    reduce_scatter x1, waiting for transfers between devices, body(): lax.psum_scatter(expert_partial.astype(jnp.bfloat16), 'tensor', scatter_d...  87.5 us
    all_gather x1, waiting for transfers between devices, body(): lax.all_gather(out_weight, 'expert', axis=1, tiled=True)  87.5 us
    all_to_all x1, waiting for transfers between devices, body(): lax.all_to_all(expert_share, 'expert', split_axis=0, concat_axis=0, tiled...  73.5 us
    all_gather x1, waiting for transfers between devices, add_all(): pieces = lax.all_gather(x, name, axis=0, tiled=False)  49.6 us
    another operation x3, other arithmetic  31.3 us
    scatter x1, local copies, waits for them, and re-layouts, body(): buffer_rows = buffer_rows.at[destination].set(normed_full[token_index])  18.2 us
    gather x1, local copies, waits for them, and re-layouts, body(): buffer_rows = buffer_rows.at[destination].set(normed_full[token_index])  16.4 us
  transfers between devices with their start and end apart: 4, of which 4 were waited for; matrix products, arithmetic and copies ran while one was open for 4% of the time, Pallas kernels for 0%

profile of v1, /device:TPU:8, one launch (start us, length us, event | category | flops | bytes accessed | tf_op | source)
XLA Modules:
  0.0 772.8 jit_solution(17334947730129627819)
XLA Ops:
  6.5 0.7 all-gather.4.cloned.1.call-update
  7.3 87.5 %all-gather.4.cloned.1.call-done = bf16[1024,4096]{0,1:T(8,128)(2,1)} async-done(((bf16[1024,64]{0,1:T(8,128)(2,1)}), bf16[1024,4096]{0,1:T(8,128)(2,1)}) %all-gather.4.cloned.1.call-update) | async-done | bytes 8388624 | tf_op jit(solution)/shard_map/all_gather | solution.py:34
  94.8 7.7 fusion.18
  102.6 0.1 copy.22
  102.9 0.7 fusion.17
  103.6 31.2 %reduce-window.6 = s32[64,8,128]{2,1,0:T(8,128)S(1)} reduce-window(s32[64,8,128]{2,1,0:T(8,128)} %fusion.17, s32[]{:T(128)} %constant.20.clone.1), window={size=1x1x128 pad=0_0x0_0x127_0}, to_apply=%region_1.0 | reduce-window | flops 8323072 | bytes 524292 | tf_op jit(solution)/shard_map/reduce-window
  134.8 0.8 slice.12
  135.6 1.1 copy.24
  136.8 0.1 copy.21
  137.1 0.1 broadcast_add_fusion
  137.3 49.6 %all-gather.6.cloned.1.call-done = f32[512,4096]{1,0:T(8,128)} async-done(((f32[128,4096]{1,0:T(8,128)}), f32[512,4096]{1,0:T(8,128)}) %all-gather.6.cloned.1.call-update) | async-done | bytes 8388624 | tf_op jit(solution)/shard_map/all_gather | solution.py:10
  187.0 5.6 reduce_sum.38
  192.5 2.3 fusion.10
  194.8 1.1 copy-done.2
  195.9 1.4 fusion.12
  197.3 16.4 %gather_fusion = bf16[1024,4096]{1,0:T(8,128)(2,1)} fusion(bf16[128,4096]{1,0:T(8,128)(2,1)} %fusion.12, s32[1024]{0:T(1024)S(1)} %broadcast_clamp_fusion.1), kind=kCustom, calls=%fused_computation | custom fusion | bytes 16781312 | tf_op jit(solution)/shard_map/gather | solution.py:55
  213.7 18.2 %scatter_custom_fusion = bf16[1152,4096]{1,0:T(8,128)(2,1)} fusion(s32[1024]{0:T(1024)S(1)} %bitcast.45, bf16[1024,4096]{1,0:T(8,128)(2,1)} %gather_fusion, bf16[]{:T(256)} %constant.39.clone.1), kind=kCustom, calls=%fused_computation.4 | custom fusion | bytes 9437696 | tf_op jit(solution)/shard_map/scatter | solution.py:55
  231.9 13.9 %reshape.114 = bf16[64,18,4096]{2,1,0:T(8,128)(2,1)} reshape(bf16[1152,4096]{1,0:T(8,128)(2,1)} %scatter_custom_fusion) | data formatting | bytes 18874368 | tf_op jit(solution)/shard_map/reshape | solution.py:56
  245.8 286.7 %all_to_all.10 = bf16[64,18,4096]{2,1,0:T(8,128)(2,1)} all-to-all(bf16[64,18,4096]{2,1,0:T(8,128)(2,1)} %reshape.114), channel_id=1, replica_groups=mesh['expert'=64,'tensor'=4] {'expert'}, dimensions={0} | all-to-all | bytes 18874368 | tf_op jit(solution)/shard_map/all_to_all | solution.py:57
  532.4 14.2 %reshape.115 = bf16[1152,4096]{1,0:T(8,128)(2,1)} reshape(bf16[64,18,4096]{2,1,0:T(8,128)(2,1)} %all_to_all.10) | data formatting | bytes 18874368 | tf_op jit(solution)/shard_map/reshape | solution.py:60
  546.7 8.7 %fusion.5 = f32[1152,384]{1,0:T(8,128)S(1)} fusion(bf16[1152,4096]{1,0:T(8,128)(2,1)} %reshape.115, bf16[1,4096,384]{2,1,0:T(8,128)(2,1)} %param.15), kind=kOutput, calls=%fused_computation.11 | convolution fusion | flops 3623878656 | bytes 14352384 | tf_op jit(solution)/shard_map/dot_general | solution.py:61
  555.4 6.2 fusion.7
  561.6 2.2 dot_general.17
  563.7 8.7 %convolution_convert_fusion = bf16[64,18,4096]{2,0,1:T(8,128)(2,1)} fusion(bf16[1,384,4096]{2,1,0:T(8,128)(2,1)S(1)} %copy-done, bf16[64,18,384]{2,1,0:T(8,128)(2,1)} %dot_general.17), kind=kOutput, calls=%fused_computation.3 | convolution fusion | flops 3628597248 | bytes 13467648 | tf_op jit(solution)/shard_map/dot_general | solution.py:64
  572.4 87.5 %reduce-scatter.2.cloned.1.call-done = bf16[64,18,1024]{2,0,1:T(8,128)(2,1)} async-done(((bf16[64,18,4096]{2,0,1:T(8,128)(2,1)}), bf16[64,18,1024]{2,0,1:T(8,128)(2,1)}) %reduce-scatter.2.cloned.1.call-update) | async-done | bytes 2359312 | tf_op jit(solution)/shard_map/reduce_scatter | solution.py:66
  660.0 4.7 copy.27
  664.7 10.9 %all-to-all-start.1 = ((bf16[64,18,1024]{2,1,0:T(8,128)(2,1)}), bf16[64,18,1024]{2,1,0:T(8,128)(2,1)}, u32[]{:S(2)}, u32[]{:S(2)}) async-start(bf16[64,18,1024]{2,1,0:T(8,128)(2,1)} %copy.27), calls=%async_computation.2 | async-start | bytes 6291456 | tf_op jit(solution)/shard_map/all_to_all | solution.py:69
  675.7 73.5 %all-to-all-done.1 = bf16[64,18,1024]{2,1,0:T(8,128)(2,1)} async-done(((bf16[64,18,1024]{2,1,0:T(8,128)(2,1)}), bf16[64,18,1024]{2,1,0:T(8,128)(2,1)}, u32[]{:S(2)}, u32[]{:S(2)}) %all-to-all-start.1) | async-done | bytes 2359328 | tf_op jit(solution)/shard_map/all_to_all | solution.py:69
  749.3 4.3 reshape.116
  753.6 8.0 %gather_fusion.1 = bf16[1024,1024]{1,0:T(8,128)(2,1)} fusion(bf16[1152,1024]{1,0:T(8,128)(2,1)} %reshape.116, s32[1024]{0:T(1024)S(1)} %broadcast_clamp_fusion), kind=kCustom, calls=%fused_computation.1 | custom fusion | bytes 4198400 | tf_op jit(solution)/shard_map/gather | solution.py:70
  761.6 2.9 fusion.2
  764.5 1.7 add_convert_fusion.1
  (33 shorter events, 0.7 us)
Async XLA Ops:
  6.5 557.2 %copy-start = (bf16[1,384,4096]{2,1,0:T(8,128)(2,1)S(1)}, bf16[1,384,4096]{2,1,0:T(8,128)(2,1)}, u32[]{:S(2)}) copy-start(bf16[1,384,4096]{2,1,0:T(8,128)(2,1)} %param.17) | copy-start | bytes 9437188
  6.5 88.3 %all-gather.4.cloned.1.call-start = ((), (), s32[]{:S(2)}) async-start(), calls=%async_computation.3 | async-start | bytes 8519680 | tf_op jit(solution)/shard_map/all_gather | solution.py:34
  7.3 95.3 %copy-start.3 = (s32[128,8]{0,1:T(8,128)S(1)}, s32[128,8]{0,1:T(8,128)}, u32[]{:S(2)}) copy-start(s32[128,8]{0,1:T(8,128)} %param.13) | copy-start | bytes 12292
  7.3 179.7 %all-gather.6.cloned.1.call-start = ((), (), s32[]{:S(2)}) async-start(), calls=%async_computation.5 | async-start | bytes 10485760 | tf_op jit(solution)/shard_map/all_gather | solution.py:10
  102.5 34.5 %copy-start.4 = (bf16[4096]{0:T(1024)(128)(2,1)S(1)}, bf16[4096]{0:T(1024)(128)(2,1)}, u32[]{:S(2)}) copy-start(bf16[4096]{0:T(1024)(128)(2,1)} %param.12) | copy-start | bytes 24580
  102.6 557.4 %reduce-scatter.2.cloned.1.call-start = ((), (), s32[]{:S(2)}) async-start(), calls=%async_computation.4 | async-start | bytes 11796480 | tf_op jit(solution)/shard_map/reduce_scatter | solution.py:66
  194.8 1.1 copy-start.2
  546.7 8.7 %copy-start.1 = (bf16[1152,4096]{1,0:T(8,128)(2,1)S(1)}, bf16[1152,4096]{1,0:T(8,128)(2,1)}, u32[]{:S(2)}) copy-start(bf16[1152,4096]{1,0:T(8,128)(2,1)} %reshape.115) | copy-start | bytes 28311556
  546.7 8.7 %copy-start.6 = (bf16[1,4096,384]{2,1,0:T(8,128)(2,1)S(1)}, bf16[1,4096,384]{2,1,0:T(8,128)(2,1)}, u32[]{:S(2)}) copy-start(bf16[1,4096,384]{2,1,0:T(8,128)(2,1)} %param.16) | copy-start | bytes 9437188
  664.7 10.9 %copy-start.5 = (f32[128,8]{0,1:T(8,128)S(1)}, f32[128,8]{0,1:T(8,128)}, u32[]{:S(2)}) copy-start(f32[128,8]{0,1:T(8,128)} %param.14) | copy-start | bytes 12292
  664.7 84.5 %all-to-all-start.1 = ((bf16[64,18,1024]{2,1,0:T(8,128)(2,1)}), bf16[64,18,1024]{2,1,0:T(8,128)(2,1)}, u32[]{:S(2)}, u32[]{:S(2)}) async-start(bf16[64,18,1024]{2,1,0:T(8,128)(2,1)} %copy.27), calls=%async_computation.2 | async-start | bytes 6291456 | tf_op jit(solution)/shard_map/all_to_all | solution.py:69
Sparse Core Ops, SparseCore 0:
  10.1 84.6 all-gather.3
  102.7 84.2 all-gather.5
  572.6 87.3 reduce-scatter.1
